TPU v7x, 512 devices: a whole 4x4x16 slice. The times are simulated.
512 devices in a mesh: dp: 64 (over x, z), tensor: 8 (over y, core).
Axes of the slice: x: 4, y: 4, z: 16, core: 2. Of those that a mesh axis runs over, the one named last changes fastest.
Arguments:
- tokens: bfloat16 [8192, 8192], P('dp', 'tensor'), may hold values from -6 to 6
- hidden_grad: bfloat16 [8192, 28672], P('dp', 'tensor'), may hold values from -0.0625 to 0.0625
- masters: float32 [8, 64, 128, 128], P('tensor', 'dp'), may hold values from -0.5 to 0.5
- block_row: int32 [8, 32], P('tensor'), may hold values from 0 to 63, as said below
- block_col: int32 [8, 32], P('tensor'), may hold values from 0 to 27
- owners: int32 [8, 64], P('tensor'), may hold values from 0 to 63, as said below
Outputs:
- grads: float32 [8, 192, 128, 128], P('tensor', 'dp')
Inputs may be any that keep to these rules, and one draw needn't show every extreme that they name: `block_row`: in each slice the kept places are distinct. `owners`: in each slice every owner takes at most 3 of the 64 kept blocks, and some owner takes exactly 3.
All inputs are finite; a program needn't handle non-finite values.
Results may differ from a plain program's by a relative error of at most 0.0044.
Values may be sent and summed in bfloat16 or wider, within the bound.
A program may use at most 64 MiB of HBM per device.

v0:
```python
import jax
import jax.numpy as jnp
from jax import lax
from jax.sharding import PartitionSpec as P


def slot_index(owner_row, capacity):
    count_all = owner_row.shape[0]
    same_owner = owner_row[:, None] == owner_row[None, :]
    earlier = (
        jnp.arange(count_all, dtype=jnp.int32)[None, :]
        < jnp.arange(count_all, dtype=jnp.int32)[:, None]
    )
    rank_index = jnp.sum(
        jnp.logical_and(same_owner, earlier).astype(jnp.int32), axis=1, dtype=jnp.int32
    )
    return owner_row * capacity + rank_index


def column_total(part, same_column):
    return jnp.einsum("tjc,kj->tkc", part, same_column, precision=lax.Precision.HIGHEST)


def local(tokens, hidden_grad, masters, block_row, block_col, owners):
    high = lax.Precision.HIGHEST
    features = lax.all_gather(tokens, "tensor", axis=1, tiled=True)
    token_count = features.shape[0]
    block_side = masters.shape[-1]
    kept_count = block_row.shape[1]
    weights = lax.all_gather(masters.astype(jnp.bfloat16), "dp", axis=1, tiled=True)[0]
    row_index = block_row[0]
    column_index = block_col[0]
    by_block = features.reshape(token_count, features.shape[1] // block_side, block_side)
    selected = jnp.take(by_block, row_index, axis=1)
    gate_part = jnp.einsum(
        "tkb,kbc->tkc", selected, weights[:kept_count], preferred_element_type=jnp.float32
    )
    up_part = jnp.einsum(
        "tkb,kbc->tkc", selected, weights[kept_count:], preferred_element_type=jnp.float32
    )
    same_column = (column_index[:, None] == column_index[None, :]).astype(jnp.float32)
    gate_value = column_total(gate_part, same_column)
    up_value = column_total(up_part, same_column)
    grad_columns = hidden_grad.reshape(token_count, hidden_grad.shape[1] // block_side, block_side)
    upstream = jnp.take(grad_columns, column_index, axis=1).astype(jnp.float32)
    sigmoid_gate = jax.nn.sigmoid(gate_value)
    gate_grad = (
        upstream * up_value * sigmoid_gate * (1.0 + gate_value * (1.0 - sigmoid_gate))
    ).astype(jnp.bfloat16)
    up_grad = (upstream * gate_value * sigmoid_gate).astype(jnp.bfloat16)
    grad_gate = jnp.einsum("tkb,tkc->kbc", selected, gate_grad, preferred_element_type=jnp.float32)
    grad_up = jnp.einsum("tkb,tkc->kbc", selected, up_grad, preferred_element_type=jnp.float32)
    block_grads = jnp.concatenate([grad_gate, grad_up], axis=0)
    owner_count = lax.axis_size("dp")
    capacity = 3 * block_grads.shape[0] // owner_count
    slot_list = slot_index(owners[0], capacity)
    summed = lax.psum(block_grads, "dp")
    own_slots = lax.axis_index("dp") * capacity + jnp.arange(capacity, dtype=jnp.int32)
    selector = (own_slots[:, None] == slot_list[None, :]).astype(jnp.float32)
    result = jnp.einsum("sk,kbc->sbc", selector, summed, precision=high)
    return result[None]


def solution(mesh):
    return jax.shard_map(
        local,
        mesh=mesh,
        in_specs=(
            P("dp", "tensor"),
            P("dp", "tensor"),
            P("tensor", "dp", None, None),
            P("tensor", None),
            P("tensor", None),
            P("tensor", None),
        ),
        out_specs=P("tensor", "dp", None, None),
        check_vma=False,
    )
```

profile of v0, /device:TPU:24, one launch (start us, length us, event | category | flops | bytes accessed | tf_op | source)
XLA Modules:
  0.0 504.8 jit_solution(9367897133489525281)
XLA Ops:
  6.5 0.0 all-gather.3.cloned.1.call-start
  6.5 1.8 copy.48
  8.3 0.0 copy-start.3
  8.3 0.0 all-gather.3.cloned.1.call-update
  8.4 0.0 all-gather.5.cloned.1.call-start
  8.4 1.5 bitcast_convert_fusion
  9.9 0.0 all-gather.5.cloned.1.call-update
  9.9 0.0 all-reduce.2.cloned.1.call-start
  10.0 1.6 copy.51
  11.5 0.0 copy-start.2
  11.5 0.6 copy.52
  12.2 0.0 copy-done.3
  12.2 1.6 gather_fusion.1
  13.9 0.0 copy-done.2
  13.9 31.7 %all-gather.3.cloned.1.call-done = bf16[128,8192]{0,1:T(8,128)(2,1)} async-done(((bf16[128,1024]{0,1:T(8,128)(2,1)}), bf16[128,8192]{0,1:T(8,128)(2,1)}) %all-gather.3.cloned.1.call-update) | async-done | bytes 2097168 | tf_op jit(solution)/shard_map/all_gather | solution.py:26
  45.6 3.2 copy.49
  48.8 0.7 gather_fusion
  49.6 0.6 fusion.24
  50.2 1.2 copy.61
  51.4 139.4 %all-gather.5.cloned.1.call-done = bf16[1,64,128,128]{3,2,0,1:T(8,128)(2,1)} async-done(((bf16[1,1,128,128]{3,2,0,1:T(8,128)(2,1)}), bf16[1,64,128,128]{3,2,0,1:T(8,128)(2,1)}) %all-gather.5.cloned.1.call-update) | async-done | bytes 2097168 | tf_op jit(solution)/shard_map/all_gather | solution.py:30
  190.9 0.0 copy-start
  190.9 1.9 convolution_bitcast_fusion
  192.8 0.0 copy-done
  192.8 0.0 copy-start.1
  192.8 0.5 convolution_bitcast_fusion.1
  193.3 0.7 copy-done.1
  194.0 3.5 fusion.9
  197.5 3.8 fusion.7
  201.3 0.8 fusion.22
  202.0 0.8 fusion.20
  202.8 2.5 pad_maximum_fusion
  205.3 0.0 copy-start.4
  205.3 0.0 all-reduce.2.cloned.1.call-update
  205.3 0.6 copy-done.4
  205.9 0.2 convert_reduce_fusion
  206.1 285.7 %all-reduce.2.cloned.1.call-done = f32[64,128,128]{2,1,0:T(8,128)} async-done(((f32[64,128,128]{2,1,0:T(8,128)}), f32[64,128,128]{2,1,0:T(8,128)}) %all-reduce.2.cloned.1.call-update) | async-done | bytes 4194320 | tf_op jit(solution)/shard_map/psum | solution.py:57
  491.8 5.8 %fusion.17 = f32[1,3,128,128]{3,1,2,0:T(4,128)S(1)} fusion(f32[64,128,128]{2,1,0:T(8,128)} %all-reduce.2.cloned.1.call-done, s32[64]{0:T(128)S(1)} %fusion.40, s32[3]{0:T(128)S(1)} %iota_add_fusion), kind=kOutput, calls=%fused_computation.24 | convolution fusion | flops 37748928 | bytes 4391180 | tf_op jit(solution)/shard_map/sk,kbc->sbc/dot_general | solution.py:60
  497.6 0.7 copy.66
  (8 shorter events, 0.0 us)
Async XLA Ops:
  6.5 39.1 %all-gather.3.cloned.1.call-start = ((), (), s32[]{:S(2)}) async-start(), calls=%async_computation | async-start | bytes 2359296 | tf_op jit(solution)/shard_map/all_gather | solution.py:26
  8.3 3.8 copy-start.3
  8.4 182.5 %all-gather.5.cloned.1.call-start = ((), (), s32[]{:S(2)}) async-start(), calls=%async_computation.1 | async-start | bytes 2129920 | tf_op jit(solution)/shard_map/all_gather | solution.py:30
  9.9 481.9 %all-reduce.2.cloned.1.call-start = ((), (), s32[]{:S(2)}) async-start(), calls=%async_computation.2 | async-start | bytes 8388608 | tf_op jit(solution)/shard_map/psum | solution.py:57
  11.5 2.3 copy-start.2
  190.9 1.9 copy-start
  192.8 1.2 copy-start.1
  205.3 0.7 copy-start.4
Sparse Core Ops, SparseCore 0:
  9.5 36.0 all-gather.2
  48.5 142.2 all-gather.4
  205.4 286.3 all-reduce.1
where the time goes:
time: 505 us
  waiting for transfers between devices  457 us (90%)
  matrix products  17 us (3%)
  between operations  13.3 us (3%)
  local copies, waits for them, and re-layouts  12.8 us (3%)
    psum x1, waiting for transfers between devices, local(): summed = lax.psum(block_grads, 'dp')  286 us
    all_gather x1, waiting for transfers between devices, local(): lax.all_gather(masters.astype(jnp.bfloat16), 'dp', axis=1, tiled=True)[0]  139 us
    all_gather x1, waiting for transfers between devices, local(): features = lax.all_gather(tokens, 'tensor', axis=1, tiled=True)  31.7 us
  transfers between devices with their start and end apart: 3, of which 3 were waited for; matrix products, arithmetic and copies ran while one was open for 2% of the time, Pallas kernels for 0%

commit v1 on v0

v1 whole, which is shorter than its diff:
```python
import functools

import jax
import jax.numpy as jnp
from jax import lax
from jax.experimental import pallas as pl
from jax.experimental.pallas import tpu as pltpu
from jax.sharding import PartitionSpec as P

MESH = pl.DeviceIdType.MESH
X, Z, Y, CORES = 4, 16, 4, 2
B = 128
KP = 32
CAP = 3
F32, BF16 = jnp.float32, jnp.bfloat16
VMEM = pl.BlockSpec(memory_space=pltpu.VMEM)
SMEM = pl.BlockSpec(memory_space=pltpu.SMEM)
DMA = pltpu.SemaphoreType.DMA
STEPS = (2, 1, -1, 0)


def place():
    dp, t = lax.axis_index("dp"), lax.axis_index("tensor")
    return dp // Z, lax.rem(dp, Z), t


def x_peer(x, z, t, step):
    return (lax.rem(x + step + X, X) * Z + z, t)


def z_peer(x, z, t, step):
    return (x * Z + lax.rem(z + step + Z, Z), t)


def y_peer(x, z, t, step):
    return (x * Z + z, lax.rem(t + CORES * step + Y * CORES, Y * CORES))


def core_peer(x, z, t):
    return (x * Z + z, t + 1 - 2 * lax.rem(t, CORES))


def meet(peers):
    barrier = pltpu.get_barrier_semaphore()
    for peer in peers:
        pl.semaphore_signal(barrier, inc=1, device_id=peer, device_id_type=MESH)
    pl.semaphore_wait(barrier, len(peers))


def send(src, dst, send_sem, recv_sem, peer):
    return pltpu.make_async_remote_copy(
        src_ref=src, dst_ref=dst, send_sem=send_sem, recv_sem=recv_sem,
        device_id=peer, device_id_type=MESH,
    )


def gather_kernel(tokens, masters, feats, weights, own, xs, xr, zs, zr, ys, yr, cs, cr):
    x, z, t = place()
    meet(
        [x_peer(x, z, t, s) for s in (1, 2, 3)]
        + [z_peer(x, z, t, s) for s in (1, -1)]
        + [y_peer(x, z, t, s) for s in (1, 2, 3)]
        + [core_peer(x, z, t)]
    )
    own[...] = masters[...].astype(BF16)
    spot = (z * 2 + lax.rem(x, 2), slice(None), pl.ds(pl.multiple_of(x // 2 * B, B), B))
    moves = []
    first = [
        send(own, weights.at[spot], xs.at[s - 1], xr.at[s - 1], x_peer(x, z, t, s))
        for s in (1, 3, 2)
    ]
    for copy in first:
        copy.start()
    y_moves = {
        s: send(tokens, feats.at[t], ys.at[s - 1], yr.at[s - 1], y_peer(x, z, t, s))
        for s in (1, 3, 2)
    }
    for copy in y_moves.values():
        copy.start()
    over = send(tokens, feats.at[t], cs.at[0], cr.at[0], core_peer(x, z, t))
    over.start()
    weights[spot] = own[...]
    feats[t] = tokens[...]
    for copy in first:
        copy.wait_recv()

    def hop(way, step, part):
        sign = 1 - 2 * way
        index = lax.rem(z - sign * step + 2 * Z, Z) * 2 + part
        return send(
            weights.at[index], weights.at[index],
            zs.at[way, step, part], zr.at[way, step, part], z_peer(x, z, t, sign),
        )

    def hops(step):
        if step < 7:
            return [(way, part) for part in (0, 1) for way in (0, 1)]
        return [(0, 0), (1, 1)]

    sent = []
    waiting = []
    for step in range(8):
        now = []
        for way, part in hops(step):
            if step:
                hop(way, step - 1, part).wait_recv()
            copy = hop(way, step, part)
            copy.start()
            now.append(copy)
        if step == 7:
            for way, part in ((0, 1), (1, 0)):
                hop(way, 6, part).wait_recv()
        sent += now
        if step in (3, 4, 5):
            s = {3: 1, 4: 3, 5: 2}[step]
            y_moves[s].wait_recv()
            source = lax.rem(t - CORES * s + Y * CORES, Y * CORES)
            copy = send(feats.at[source], feats.at[source], cs.at[s], cr.at[s], core_peer(x, z, t))
            copy.start()
            waiting.append(copy)
    for copy in now:
        copy.wait_recv()
    over.wait_recv()
    for copy in waiting:
        copy.wait_recv()
    for copy in sent + first + list(y_moves.values()) + [over] + waiting:
        copy.wait_send()


def compute_kernel(meta, keep, feats, weights, hidden, out, part, grads):
    def selected(i):
        return feats[meta[0, i], :, pl.ds(pl.multiple_of(meta[1, i], B), B)]

    def forward(i):
        value = jnp.dot(selected(i), weights[meta[2, i]], preferred_element_type=F32)
        part[i + 1] = part[i] * keep[i] + value

    part[0] = jnp.zeros_like(part[0])

    @pl.loop(0, KP, unroll=4)
    def _(i):
        forward(i)

    def backward(i):
        last = meta[3, i]
        gate = part[last, :, :B]
        up = part[last, :, B:]
        upstream = hidden[:, pl.ds(pl.multiple_of(meta[4, i], B), B)].astype(F32)
        sig = 1.0 / (1.0 + jnp.exp(-gate))
        gate_grad = upstream * up * sig * (1.0 + gate * (1.0 - sig))
        up_grad = upstream * gate * sig
        grads[:, :B] = gate_grad.astype(BF16)
        grads[:, B:] = up_grad.astype(BF16)
        total = lax.dot_general(
            selected(i), grads[...], (((0,), (0,)), ((), ())), preferred_element_type=F32
        )
        at = pl.ds(pl.multiple_of(i * 16, 16), 16)
        for p in range(16):
            rows = total[8 * p : 8 * p + 8]
            out[p, at] = jnp.concatenate([rows[:, :B], rows[:, B:]], axis=0).astype(BF16)

    @pl.loop(0, KP, unroll=2)
    def _(i):
        backward(i)


def reduce_kernel(
    inverse, partial, out, got, near_out, near_in, mine, owner_out, owner_in, final_out,
    xs, xr, ns, nr, os, ors, fs, fr,
):
    x, z, t = place()
    meet(
        [x_peer(x, z, t, s) for s in (1, 2, 3)]
        + [z_peer(x, z, t, s) for s in range(1, Z)]
    )
    half = KP * 8

    def x_copy(j, s):
        piece = lax.rem(x + s, X) * 4 + lax.rem(z + STEPS[j] + Z, 4)
        return send(
            partial.at[piece], got.at[j, s - 1], xs.at[j, s - 1], xr.at[j, s - 1],
            x_peer(x, z, t, s),
        )

    x_copies = [[x_copy(j, s) for s in (1, 3, 2)] for j in range(4)]
    for row in x_copies:
        for copy in row:
            copy.start()

    def near_copies(j):
        if j == 0:
            return [
                send(near_out.at[0, pl.ds(0, half)], near_in.at[0, pl.ds(0, half)],
                     ns.at[0], nr.at[0], z_peer(x, z, t, 2)),
                send(near_out.at[0, pl.ds(half, half)], near_in.at[0, pl.ds(half, half)],
                     ns.at[3], nr.at[3], z_peer(x, z, t, -2)),
            ]
        return [send(near_out.at[j], near_in.at[j], ns.at[j], nr.at[j], z_peer(x, z, t, STEPS[j]))]

    near = []
    tile = 64
    for j in range(4):
        for copy in x_copies[j]:
            copy.wait_recv()
        piece = x * 4 + lax.rem(z + STEPS[j] + Z, 4)

        @pl.loop(0, 2 * half // tile)
        def _(r):
            at = pl.ds(pl.multiple_of(r * tile, tile), tile)
            total = partial[piece, at].astype(F32)
            for s in range(3):
                total += got[j, s, at].astype(F32)
            if j < 3:
                near_out[j, at] = total.astype(BF16)
            else:
                mine[pl.ds(r * 8, 8)] = total.reshape(8, 8, B)

        if j < 3:
            for copy in near_copies(j):
                copy.start()
                near.append(copy)
    for copy in near:
        copy.wait_recv()

    @pl.loop(0, 2 * half // tile)
    def _(r):
        at = pl.ds(pl.multiple_of(r * tile, tile), tile)
        blocks = pl.ds(r * 8, 8)
        total = mine[blocks].reshape(tile, B)
        for j in range(3):
            total += near_in[j, at].astype(F32)
        mine[blocks] = total.reshape(8, 8, B)

    mine[2 * KP] = jnp.zeros((8, B), F32)

    def slot(zo, q):
        number = (q // CAP * Z + zo) * CAP + q % CAP
        return mine[inverse[number]]

    owner_copies = []
    for step in [8, 7, 9, 6, 10, 5, 11, 4, 12, 3, 13, 2, 14, 1, 15, 0]:
        zo = lax.rem(z + step, Z)
        for q in range(0, 12, 2):
            owner_out[step, 8 * q : 8 * q + 16] = jnp.concatenate(
                [slot(zo, q), slot(zo, q + 1)], axis=0
            ).astype(BF16)
        if step:
            copy = send(owner_out.at[step], owner_in.at[step], os.at[step], ors.at[step],
                        z_peer(x, z, t, step))
            copy.start()
            owner_copies.append(copy)
    for copy in owner_copies:
        copy.wait_recv()
    for e in range(4):
        total = owner_out[0] if e == 0 else owner_in[e]
        total = total.astype(F32)
        for k in (4, 8, 12):
            total += owner_in[e + k].astype(F32)
        row = pl.multiple_of(lax.rem(z - e + Z, 4) * 8, 8)
        for q in range(12):
            final_out[q // CAP, q % CAP, pl.ds(row, 8)] = total[8 * q : 8 * q + 8]
    rows = pl.ds(pl.multiple_of(x * 32, 32), 32)
    final = [
        send(final_out.at[lax.rem(x + s, X)], out.at[:, rows], fs.at[s - 1], fr.at[s - 1],
             x_peer(x, z, t, s))
        for s in (1, 3, 2)
    ]
    for copy in final:
        copy.start()
    out[:, rows] = final_out[x]
    for copy in final:
        copy.wait_recv()
    for copy in sum(x_copies, []) + near + owner_copies + final:
        copy.wait_send()


def tables(rows, columns, owners):
    places = jnp.arange(KP, dtype=jnp.int32)
    before = (columns[None, :] < columns[:, None]) | (
        (columns[None, :] == columns[:, None]) & (places[None, :] < places[:, None])
    )
    rank = jnp.sum(before.astype(jnp.int32), axis=1)
    hit = (rank[None, :] == places[:, None]).astype(jnp.int32)
    order = jnp.sum(hit * places[None, :], axis=1)
    row = jnp.sum(hit * rows[None, :], axis=1)
    column = jnp.sum(hit * columns[None, :], axis=1)
    upto = jnp.sum((columns[None, :] <= column[:, None]).astype(jnp.int32), axis=1)
    first = jnp.sum((columns[None, :] < column[:, None]).astype(jnp.int32), axis=1)
    keep = (first != places).astype(F32)
    meta = jnp.stack(
        [row // 8, row % 8 * B, order % Z * 2 + order // Z, upto, column * B]
    )
    blocks = jnp.arange(2 * KP, dtype=jnp.int32)
    earlier = (owners[None, :] == owners[:, None]) & (blocks[None, :] < blocks[:, None])
    slots = owners * CAP + jnp.sum(earlier.astype(jnp.int32), axis=1)
    position = jnp.concatenate([rank * 2, rank * 2 + 1])
    taken = slots[None, :] == jnp.arange(X * Z * CAP, dtype=jnp.int32)[:, None]
    inverse = jnp.sum(jnp.where(taken, position[None, :] - 2 * KP, 0), axis=1) + 2 * KP
    return meta, keep, inverse


def local(tokens, hidden_grad, masters, block_row, block_col, owners):
    meta, keep, inverse = tables(block_row[0], block_col[0], owners[0])
    limit = 56 << 20
    feats, weights = pl.pallas_call(
        gather_kernel,
        name="gather",
        out_shape=[
            jax.ShapeDtypeStruct((Y * CORES, B, 8 * B), BF16),
            jax.ShapeDtypeStruct((KP, B, 2 * B), BF16),
        ],
        in_specs=[VMEM, VMEM],
        out_specs=[VMEM, VMEM],
        scratch_shapes=[pltpu.VMEM((B, B), BF16), DMA((3,)), DMA((3,)), DMA((2, 8, 2)), DMA((2, 8, 2)),
                        DMA((3,)), DMA((3,)), DMA((4,)), DMA((4,))],
        compiler_params=pltpu.CompilerParams(
            collective_id=0, has_side_effects=True, vmem_limit_bytes=limit
        ),
    )(tokens, masters.reshape(B, B))
    partial = pl.pallas_call(
        compute_kernel,
        name="compute",
        out_shape=jax.ShapeDtypeStruct((16, KP * 16, B), BF16),
        in_specs=[SMEM, SMEM, VMEM, VMEM, VMEM],
        out_specs=VMEM,
        scratch_shapes=[pltpu.VMEM((KP + 1, B, 2 * B), F32), pltpu.VMEM((B, 2 * B), BF16)],
        compiler_params=pltpu.CompilerParams(vmem_limit_bytes=limit),
    )(meta, keep, feats, weights, hidden_grad)
    size = KP * 16
    result = pl.pallas_call(
        reduce_kernel,
        name="reduce",
        out_shape=jax.ShapeDtypeStruct((CAP, B, B), F32),
        in_specs=[SMEM, VMEM],
        out_specs=VMEM,
        scratch_shapes=[
            pltpu.VMEM((4, 3, size, B), BF16),
            pltpu.VMEM((3, size, B), BF16),
            pltpu.VMEM((3, size, B), BF16),
            pltpu.VMEM((2 * KP + 1, 8, B), F32),
            pltpu.VMEM((Z, 96, B), BF16),
            pltpu.VMEM((Z, 96, B), BF16),
            pltpu.VMEM((X, CAP, 32, B), F32),
            DMA((4, 3)), DMA((4, 3)), DMA((4,)), DMA((4,)), DMA((Z,)), DMA((Z,)), DMA((3,)), DMA((3,)),
        ],
        compiler_params=pltpu.CompilerParams(
            collective_id=1, has_side_effects=True, vmem_limit_bytes=limit
        ),
    )(inverse, partial)
    return result[None]


def solution(mesh):
    return jax.shard_map(
        local,
        mesh=mesh,
        in_specs=(
            P("dp", "tensor"),
            P("dp", "tensor"),
            P("tensor", "dp", None, None),
            P("tensor", None),
            P("tensor", None),
            P("tensor", None),
        ),
        out_specs=P("tensor", "dp", None, None),
        check_vma=False,
    )
```

time: 505 us -> 118 us (0.23)
  waiting for transfers between devices: 457 us -> 0 us
  Pallas kernels: 0 us -> 111 us
  matrix products: 17 us -> 0 us
  between operations: 13.3 us -> 0.05 us
  local copies, waits for them, and re-layouts: 12.8 us -> 2.23 us
    psum x1 -> x0, waiting for transfers between devices: 286 us -> none  [local(): summed = lax.psum(block_grads, 'dp')]
    all_gather x2 -> x0, waiting for transfers between devices: 171 us -> none  [the longest x1 139 us: local(): lax.all_gather(masters.astype(jnp.bfloat16), 'dp', axis=1, tiled=True)[0]]
    pallas_call x0 -> x3, Pallas kernels: none -> 111 us  [the longest x1 50.6 us: local(): pl.pallas_call(gather_kernel, name='gather', out_shape=[jax.ShapeDtypeStr...]
    dot_general x7 -> x0, matrix products: 17 us -> none  [the longest x2 7.28 us: column_total(): jnp.einsum('tjc,kj->tkc', part, same_column, precision=lax.Precision.HIGH...]
  transfers between devices with their start and end apart: 3 -> 0, of which waited for: 3 -> 0; matrix products, arithmetic and copies ran while one was open for 2% -> 0% of each run, Pallas kernels for 0% -> 0%
where the time goes in v1:
time: 118 us; the launch traced here: 117 us
  Pallas kernels  111 us (94%)
  other arithmetic  4.05 us (3%)
  local copies, waits for them, and re-layouts  2.23 us (2%)
    pallas_call x1, Pallas kernels, local(): pl.pallas_call(gather_kernel, name='gather', out_shape=[jax.ShapeDtypeStr...  50.6 us
    pallas_call x1, Pallas kernels, local(): pl.pallas_call(reduce_kernel, name='reduce', out_shape=jax.ShapeDtypeStru...  50 us
    pallas_call x1, Pallas kernels, local(): pl.pallas_call(compute_kernel, name='compute', out_shape=jax.ShapeDtypeSt...  10.1 us

profile of v1, /device:TPU:24, one launch (start us, length us, event | category | flops | bytes accessed | tf_op | source)
XLA Modules:
  0.0 117.1 jit_solution(3099760742752431569)
XLA Ops:
  0.0 0.9 convert_reduce_fusion.3
  0.9 0.8 select_reduce_fusion.1
  1.8 0.8 convert_reduce_fusion.1
  2.6 0.6 stack.5.meta
  3.2 0.5 compare_convert_fusion.keep
  3.7 50.6 %gather.1 = (bf16[8,128,1024]{2,1,0:T(8,128)(2,1)}, bf16[32,128,256]{2,1,0:T(8,128)(2,1)}) custom-call(bf16[128,1024]{1,0:T(8,128)(2,1)} %tokens.1, f32[128,128]{1,0:T(8,128)} %bitcast.43), custom_call_target="tpu_custom_call" | custom-call | tf_op jit(solution)/shard_map/gather/pallas_call | solution.py:305
  54.3 0.0 copy-start
  54.4 10.1 %compute.1.partial = bf16[16,512,128]{2,1,0:T(8,128)(2,1)} custom-call(s32[5,32]{1,0:T(8,128)} %stack.5.meta, f32[32]{0:T(128)} %compare_convert_fusion.keep, bf16[8,128,1024]{2,1,0:T(8,128)(2,1)} %get-tuple-element.7.feats, bf16[32,128,256]{2,1,0:T(8,128)(2,1)} %get-tuple-element.8.weights, bf16[128,3584]{1,0:T(8,128)(2,1)} %hidden.1), custom_call_target="tpu_custom_call" | custom-call | tf_op jit(solution)/shard_map/compute/pallas_call | solution.py:320
  64.5 0.1 add_add_fusion
  64.6 0.0 copy-done
  64.6 0.2 convert_reduce_fusion
  64.8 0.1 select_reduce_fusion
  64.9 0.6 broadcast_add_fusion.inverse
  65.4 50.0 %reduce.1 = f32[3,128,128]{2,1,0:T(8,128)} custom-call(s32[192]{0:T(256)} %broadcast_add_fusion.inverse, bf16[16,512,128]{2,1,0:T(8,128)(2,1)} %compute.1.partial), custom_call_target="tpu_custom_call" | custom-call | tf_op jit(solution)/shard_map/reduce/pallas_call | solution.py:330
  115.5 1.6 %copy.8 = f32[1,3,128,128]{3,2,1,0:T(8,128)} copy(f32[1,3,128,128]{3,2,1,0:T(8,128)} %bitcast.42) | data formatting | bytes 393216
  (4 shorter events, 0.0 us)
Async XLA Ops:
  54.3 10.2 %copy-start = (s32[1,64]{1,0:T(1,128)S(1)}, s32[1,64]{1,0:T(1,128)}, u32[]{:S(2)}) copy-start(s32[1,64]{1,0:T(1,128)} %param.11) | copy-start | bytes 772

commit v2 on v1

v2 whole, which is shorter than its diff:
```python
import functools

import jax
import jax.numpy as jnp
from jax import lax
from jax.experimental import pallas as pl
from jax.experimental.pallas import tpu as pltpu
from jax.sharding import PartitionSpec as P

MESH = pl.DeviceIdType.MESH
X, Z, Y, CORES = 4, 16, 4, 2
B = 128
KP = 32
CAP = 3
F32, BF16 = jnp.float32, jnp.bfloat16
VMEM = pl.BlockSpec(memory_space=pltpu.VMEM)
SMEM = pl.BlockSpec(memory_space=pltpu.SMEM)
DMA = pltpu.SemaphoreType.DMA
STEPS = (2, 1, -1, 0)
XSTEPS = (2, 1, 3, 0)
HALF = KP // 2


def place():
    dp, t = lax.axis_index("dp"), lax.axis_index("tensor")
    return dp // Z, lax.rem(dp, Z), t


def x_peer(x, z, t, step):
    return (lax.rem(x + step + X, X) * Z + z, t)


def z_peer(x, z, t, step):
    return (x * Z + lax.rem(z + step + Z, Z), t)


def y_peer(x, z, t, step):
    return (x * Z + z, lax.rem(t + CORES * step + Y * CORES, Y * CORES))


def core_peer(x, z, t):
    return (x * Z + z, t + 1 - 2 * lax.rem(t, CORES))


def greet(peers):
    barrier = pltpu.get_barrier_semaphore()
    for peer in peers:
        pl.semaphore_signal(barrier, inc=1, device_id=peer, device_id_type=MESH)
    return lambda: pl.semaphore_wait(barrier, len(peers))


def send(src, dst, send_sem, recv_sem, peer):
    return pltpu.make_async_remote_copy(
        src_ref=src, dst_ref=dst, send_sem=send_sem, recv_sem=recv_sem,
        device_id=peer, device_id_type=MESH,
    )


def total(mask, values, axis):
    return jnp.sum(jnp.where(mask, values, 0), axis=axis, keepdims=True)


def tables(rows, columns, owners):
    i32 = jnp.int32

    def grid(a, b, dim):
        return lax.broadcasted_iota(i32, (a, b), dim)

    sub, lane = grid(KP, KP, 0), grid(KP, KP, 1)
    col_t, row_t = total(sub == lane, columns, 1), total(sub == lane, rows, 1)
    before = (columns < col_t) | ((columns == col_t) & (lane < sub))
    rank_t = jnp.sum(before.astype(i32), axis=1, keepdims=True)
    sub, lane = grid(KP, B, 0), grid(KP, B, 1)
    hit = rank_t == lane
    order = total(hit, sub, 0)
    row_s = total(hit, row_t, 0)
    col_s = total(hit, col_t, 0)
    upto = jnp.sum((col_t <= col_s).astype(i32), axis=0, keepdims=True)
    first = jnp.sum((col_t < col_s).astype(i32), axis=0, keepdims=True)
    keep = (first != lax.broadcasted_iota(i32, (1, B), 1)).astype(i32)
    n = 2 * KP
    sub, lane = grid(n, n, 0), grid(n, n, 1)
    own_t = total(sub == lane, owners, 1)
    earlier = (owners == own_t) & (lane < sub)
    slot_t = own_t * CAP + jnp.sum(earlier.astype(i32), axis=1, keepdims=True)
    sub, lane = grid(n, KP, 0), grid(n, KP, 1)
    which = lax.rem(sub, KP)
    col_n = total(which == lane, columns, 1)
    before = (columns < col_n) | ((columns == col_n) & (lane < which))
    position = 2 * jnp.sum(before.astype(i32), axis=1, keepdims=True)
    position += (grid(n, 1, 0) >= KP).astype(i32)
    taken = slot_t == grid(n, 2 * B, 1)
    inverse = n + total(taken, position - n, 0)
    return order, row_s, col_s, upto, keep, inverse


def fused(
    tokens, hidden, masters, rows, columns, owners, out,
    own, feats, weights, hidden_raw, hid, table, meta, raw, part, grads,
    part_a, part_b, in_a, in_b, out_a, out_b, in_a2, in_b2, mine, owner_out, owner_in, final_out,
    local_sem, xs, xr, zs, zr, ys, yr, cs, cr,
    as_, ar, bs, br, as2, ar2, bs2, br2, os, ors, fs, fr,
):
    x, z, t = place()
    wait_all = greet(
        [x_peer(x, z, t, s) for s in (1, 2, 3)]
        + [z_peer(x, z, t, s) for s in range(1, Z)]
        + [y_peer(x, z, t, s) for s in (1, 2, 3)]
        + [core_peer(x, z, t)]
    )
    bring = pltpu.make_async_copy(hidden, hidden_raw, local_sem.at[0])
    bring.start()
    own[...] = masters[...].astype(BF16)
    spot = (z * 2 + lax.rem(x, 2), slice(None), pl.ds(pl.multiple_of(x // 2 * B, B), B))
    weights[spot] = own[...]
    for j in range(8):
        feats[t * 8 + j] = tokens[:, j * B : j * B + B]
    my_feats = feats.at[pl.ds(t * 8, 8)]
    wait_all()

    first = [
        send(own, weights.at[spot], xs.at[s - 1], xr.at[s - 1], x_peer(x, z, t, s))
        for s in (1, 3, 2)
    ]
    for copy in first:
        copy.start()
    y_moves = {
        s: send(my_feats, my_feats, ys.at[s - 1], yr.at[s - 1], y_peer(x, z, t, s))
        for s in (1, 3, 2)
    }
    for copy in y_moves.values():
        copy.start()
    over = send(my_feats, my_feats, cs.at[0], cr.at[0], core_peer(x, z, t))
    over.start()

    order, row_s, col_s, upto, keep, inverse = tables(rows[...], columns[...], owners[...])
    for r, value in enumerate((order, row_s, col_s, upto, keep)):
        table[r : r + 1, :B] = value
    table[5:6, :] = inverse
    table[6:7, :KP] = rows[...]
    to_scalar = pltpu.make_async_copy(table, meta, local_sem.at[1])
    to_scalar.start()

    for copy in first:
        copy.wait_recv()

    def hop(way, step, half):
        sign = 1 - 2 * way
        index = lax.rem(z - sign * step + 2 * Z, Z) * 2 + half
        return send(
            weights.at[index], weights.at[index],
            zs.at[way, step, half], zr.at[way, step, half], z_peer(x, z, t, sign),
        )

    def hops(step):
        if step < 7:
            return [(way, half) for half in (0, 1) for way in (0, 1)]
        return [(0, 0), (1, 1)]

    def forward(step, half):
        zz = lax.rem(z + step + 2 * Z, Z)
        spot_k = half * Z + zz
        raw[spot_k] = jnp.dot(
            feats[meta[6, spot_k]], weights[zz * 2 + half], preferred_element_type=F32
        )

    sent = []
    passed = []
    for step in range(8):
        now = []
        for way, half in hops(step):
            if step:
                hop(way, step - 1, half).wait_recv()
            copy = hop(way, step, half)
            copy.start()
            now.append(copy)
        if step == 7:
            for way, half in ((0, 1), (1, 0)):
                hop(way, 6, half).wait_recv()
        sent += now
        if step == 0:
            bring.wait()
            for c in range(hid.shape[0]):
                hid[c] = hidden_raw[:, c * B : c * B + B]
        if step == 1:
            to_scalar.wait()
        if step in (3, 4, 5):
            s = {3: 1, 4: 3, 5: 2}[step]
            y_moves[s].wait_recv()
            source = feats.at[pl.ds(lax.rem(t - CORES * s + Y * CORES, Y * CORES) * 8, 8)]
            copy = send(source, source, cs.at[s], cr.at[s], core_peer(x, z, t))
            copy.start()
            passed.append(copy)
        if step == 6:
            over.wait_recv()
            for copy in passed:
                copy.wait_recv()
        if step >= 6:
            early = [0, 1, -1, 2, -2, 3, -3] if step == 6 else [4, -4, 5, -5, 6, -6, 7, -7]
            for distance in early:
                for half in range(2):
                    forward(distance, half)
    for copy in now:
        copy.wait_recv()
    for half in range(2):
        forward(8, half)

    part[0] = jnp.zeros_like(part[0])

    @pl.loop(0, KP)
    def _(i):
        part[i + 1] = part[i] * meta[4, i].astype(F32) + raw[meta[0, i]]

    def backward(i, store):
        last = meta[3, i]
        value = part[last]
        gate, up = value[:, :B], value[:, B:]
        upstream = hid[meta[2, i]].astype(F32)
        sig = 1.0 / (1.0 + jnp.exp(-gate))
        scaled = upstream * sig
        grads[:, :B] = (scaled * up * (1.0 + gate * (1.0 - sig))).astype(BF16)
        grads[:, B:] = (scaled * gate).astype(BF16)
        block = lax.dot_general(
            feats[meta[1, i]], grads[...], (((0,), (0,)), ((), ())), preferred_element_type=F32
        )
        for p in range(16):
            r = block[8 * p : 8 * p + 8]
            store(p, jnp.concatenate([r[:, :B], r[:, B:]], axis=0).astype(BF16))

    @pl.loop(0, HALF)
    def _(i):
        at = pl.ds(pl.multiple_of(i * 16, 16), 16)

        def store(p, v):
            part_a[p, at] = v

        backward(i, store)

    def a_copy(j, s):
        piece = lax.rem(x + s, X) * 4 + lax.rem(z + STEPS[j] + Z, 4)
        return send(
            part_a.at[piece], in_a.at[j, s - 1], as_.at[j, s - 1], ar.at[j, s - 1],
            x_peer(x, z, t, s),
        )

    a_copies = [[a_copy(j, s) for s in (1, 3, 2)] for j in range(4)]
    for group in a_copies:
        for copy in group:
            copy.start()

    @pl.loop(0, HALF)
    def _(i):
        at = pl.ds(pl.multiple_of(i * 16, 16), 16)

        def store(p, v):
            part_b[p, at] = v

        backward(i + HALF, store)

    def b_copy(j, k):
        step = STEPS[k] if k or j % 2 == 0 else -STEPS[k]
        piece = lax.rem(x + XSTEPS[j], X) * 4 + lax.rem(z + step + Z, 4)
        return send(
            part_b.at[piece], in_b.at[j, k], bs.at[j, k], br.at[j, k], z_peer(x, z, t, step)
        )

    b_copies = [[b_copy(j, k) for k in (0, 1, 2)] for j in range(4)]
    for group in b_copies:
        for copy in group:
            copy.start()

    tile = 64
    size = HALF * 16

    def merge(own_piece, arrived, store):
        @pl.loop(0, size // tile)
        def _(r):
            at = pl.ds(pl.multiple_of(r * tile, tile), tile)
            value = own_piece[at].astype(F32)
            for k in range(3):
                value += arrived[k, at].astype(F32)
            store(r, at, value)

    second = []
    for j in range(4):
        def keep_a(r, at, value, j=j):
            if j < 3:
                out_a[j, at] = value.astype(BF16)
            else:
                mine[pl.ds(r * 8, 8)] = value.reshape(8, 8, B)

        def keep_b(r, at, value, j=j):
            if j < 3:
                out_b[j, at] = value.astype(BF16)
            else:
                mine[pl.ds(KP + r * 8, 8)] = value.reshape(8, 8, B)

        for copy in a_copies[j]:
            copy.wait_recv()
        merge(part_a.at[x * 4 + lax.rem(z + STEPS[j] + Z, 4)], in_a.at[j], keep_a)
        if j < 3:
            if j == 0:
                cut = size // 2
                pieces = [(pl.ds(0, cut), 0, 2), (pl.ds(cut, cut), 3, -2)]
            else:
                pieces = [(pl.ds(0, size), j, STEPS[j])]
            for at, sem, step in pieces:
                copy = send(out_a.at[j, at], in_a2.at[j, at], as2.at[sem], ar2.at[sem],
                            z_peer(x, z, t, step))
                copy.start()
                second.append(copy)
        for copy in b_copies[j]:
            copy.wait_recv()
        merge(part_b.at[lax.rem(x + XSTEPS[j], X) * 4 + lax.rem(z, 4)], in_b.at[j], keep_b)
        if j < 3:
            copy = send(out_b.at[j], in_b2.at[j], bs2.at[j], br2.at[j], x_peer(x, z, t, XSTEPS[j]))
            copy.start()
            second.append(copy)
    for copy in second:
        copy.wait_recv()

    for base, arrived in ((0, in_a2), (KP, in_b2)):
        @pl.loop(0, size // tile)
        def _(r):
            at = pl.ds(pl.multiple_of(r * tile, tile), tile)
            blocks = pl.ds(base + r * 8, 8)
            value = mine[blocks].reshape(tile, B)
            for j in range(3):
                value += arrived[j, at].astype(F32)
            mine[blocks] = value.reshape(8, 8, B)

    mine[2 * KP] = jnp.zeros((8, B), F32)

    def slot(zo, q):
        return mine[meta[5, (q // CAP * Z + zo) * CAP + q % CAP]]

    owner_copies = []
    for step in (8, 7, 9, 6, 10, 5, 11, 4, 12, 3, 13, 2, 14, 1, 15, 0):
        zo = lax.rem(z + step, Z)
        for q in range(0, 12, 2):
            owner_out[step, 8 * q : 8 * q + 16] = jnp.concatenate(
                [slot(zo, q), slot(zo, q + 1)], axis=0
            ).astype(BF16)
        if step:
            copy = send(owner_out.at[step], owner_in.at[step], os.at[step], ors.at[step],
                        z_peer(x, z, t, step))
            copy.start()
            owner_copies.append(copy)
    for copy in owner_copies:
        copy.wait_recv()
    for e in range(4):
        value = owner_out[0] if e == 0 else owner_in[e]
        value = value.astype(F32)
        for k in (4, 8, 12):
            value += owner_in[e + k].astype(F32)
        row = pl.multiple_of(lax.rem(z - e + Z, 4) * 8, 8)
        for q in range(12):
            final_out[q // CAP, q % CAP, pl.ds(row, 8)] = value[8 * q : 8 * q + 8]
    block_rows = pl.ds(pl.multiple_of(x * 32, 32), 32)
    final = [
        send(final_out.at[lax.rem(x + s, X)], out.at[:, block_rows], fs.at[s - 1], fr.at[s - 1],
             x_peer(x, z, t, s))
        for s in (1, 3, 2)
    ]
    for copy in final:
        copy.start()
    out[:, block_rows] = final_out[x]
    for copy in final:
        copy.wait_recv()
    done = first + list(y_moves.values()) + [over] + passed + sent
    done += sum(a_copies, []) + sum(b_copies, []) + second + owner_copies + final
    for copy in done:
        copy.wait_send()


def local(tokens, hidden_grad, masters, block_row, block_col, owners):
    size = HALF * 16
    columns = hidden_grad.shape[1] // B
    result = pl.pallas_call(
        fused,
        name="fused",
        out_shape=jax.ShapeDtypeStruct((CAP, B, B), F32),
        in_specs=[VMEM, pl.BlockSpec(memory_space=pl.ANY), VMEM, VMEM, VMEM, VMEM],
        out_specs=VMEM,
        scratch_shapes=[
            pltpu.VMEM((B, B), BF16),
            pltpu.VMEM((Y * CORES * 8, B, B), BF16),
            pltpu.VMEM((KP, B, 2 * B), BF16),
            pltpu.VMEM(hidden_grad.shape, BF16),
            pltpu.VMEM((columns, B, B), BF16),
            pltpu.VMEM((8, 2 * B), jnp.int32),
            pltpu.SMEM((8, 2 * B), jnp.int32),
            pltpu.VMEM((KP, B, 2 * B), F32),
            pltpu.VMEM((KP + 1, B, 2 * B), F32),
            pltpu.VMEM((B, 2 * B), BF16),
            pltpu.VMEM((16, size, B), BF16),
            pltpu.VMEM((16, size, B), BF16),
            pltpu.VMEM((4, 3, size, B), BF16),
            pltpu.VMEM((4, 3, size, B), BF16),
            pltpu.VMEM((3, size, B), BF16),
            pltpu.VMEM((3, size, B), BF16),
            pltpu.VMEM((3, size, B), BF16),
            pltpu.VMEM((3, size, B), BF16),
            pltpu.VMEM((2 * KP + 1, 8, B), F32),
            pltpu.VMEM((Z, 96, B), BF16),
            pltpu.VMEM((Z, 96, B), BF16),
            pltpu.VMEM((X, CAP, 32, B), F32),
            DMA((2,)),
            DMA((3,)), DMA((3,)), DMA((2, 8, 2)), DMA((2, 8, 2)), DMA((3,)), DMA((3,)), DMA((4,)), DMA((4,)),
            DMA((4, 3)), DMA((4, 3)), DMA((4, 3)), DMA((4, 3)), DMA((4,)), DMA((4,)), DMA((3,)), DMA((3,)),
            DMA((Z,)), DMA((Z,)), DMA((3,)), DMA((3,)),
        ],
        compiler_params=pltpu.CompilerParams(
            collective_id=0, has_side_effects=True, vmem_limit_bytes=56 << 20
        ),
    )(tokens, hidden_grad, masters.reshape(B, B), block_row, block_col, owners)
    return result[None]


def solution(mesh):
    return jax.shard_map(
        local,
        mesh=mesh,
        in_specs=(
            P("dp", "tensor"),
            P("dp", "tensor"),
            P("tensor", "dp", None, None),
            P("tensor", None),
            P("tensor", None),
            P("tensor", None),
        ),
        out_specs=P("tensor", "dp", None, None),
        check_vma=False,
    )
```

time: 118 us -> 99 us (0.84)
  Pallas kernels: 111 us -> 95.8 us
  other arithmetic: 4.05 us -> 0 us
    pallas_call x3 -> x1, Pallas kernels: 111 us -> 95.8 us  [local(): pl.pallas_call(fused, name='fused', out_shape=jax.ShapeDtypeStruct((CAP,...]
    reduce_sum x5 -> x0, other arithmetic: 2.85 us -> none  [the longest x1 0.91 us: tables(): rank = jnp.sum(before.astype(jnp.int32), axis=1)]
where the time goes in v2:
time: 99 us; the launch traced here: 97.4 us
  Pallas kernels  95.8 us (97%)
  local copies, waits for them, and re-layouts  1.62 us (2%)
    pallas_call x1, Pallas kernels, local(): pl.pallas_call(fused, name='fused', out_shape=jax.ShapeDtypeStruct((CAP,...  95.8 us

profile of v2, /device:TPU:24, one launch (start us, length us, event | category | flops | bytes accessed | tf_op | source)
XLA Modules:
  0.0 97.4 jit_solution(11974714012329986609)
XLA Ops:
  0.0 95.8 %fused.1 = f32[3,128,128]{2,1,0:T(8,128)} custom-call(bf16[128,1024]{1,0:T(8,128)(2,1)} %tokens.1, bf16[128,3584]{1,0:T(8,128)(2,1)} %hidden.1, f32[128,128]{1,0:T(8,128)} %bitcast.3, s32[1,32]{1,0:T(1,128)} %rows.1, s32[1,32]{1,0:T(1,128)} %columns.1, s32[1,64]{1,0:T(1,128)} %owners.1), custom_call_target="tpu_custom_call" | custom-call | tf_op jit(solution)/shard_map/fused/pallas_call | solution.py:379
  95.8 1.6 %copy.8 = f32[1,3,128,128]{3,2,1,0:T(8,128)} copy(f32[1,3,128,128]{3,2,1,0:T(8,128)} %bitcast.2) | data formatting | bytes 393216

commit v3 on v2

--- a/solution.py
+++ b/solution.py
@@ -19,6 +19,14 @@
 STEPS = (2, 1, -1, 0)
 XSTEPS = (2, 1, 3, 0)
 HALF = KP // 2
+LOW = 32
+MOVES = (
+    (0, 5), (0, -5), (0, 1), (0, -1),
+    (-5, 1), (-5, -1), (5, 1), (5, -1), (-1, 1), (1, -1),
+    (-6, 1), (4, 1), (-4, -1), (6, -1),
+    (-7, 1), (7, -1),
+)
+STAGES = ((0, 1, 2, 3), (4, 5, 6, 7, 8, 9), (10, 11, 12, 13), (14, 15))
 
 
 def place():
@@ -96,42 +104,84 @@
 
 def fused(
     tokens, hidden, masters, rows, columns, owners, out,
-    own, feats, weights, hidden_raw, hid, table, meta, raw, part, grads,
+    own, feats, low, high, hidden_raw, hid, table, meta, raw, part, grads,
     part_a, part_b, in_a, in_b, out_a, out_b, in_a2, in_b2, mine, owner_out, owner_in, final_out,
-    local_sem, xs, xr, zs, zr, ys, yr, cs, cr,
+    local_sem, xs, xr, zs, zr, hs, hr, hxs, hxr, ys, yr, cs, cr,
     as_, ar, bs, br, as2, ar2, bs2, br2, os, ors, fs, fr,
 ):
     x, z, t = place()
     wait_all = greet(
         [x_peer(x, z, t, s) for s in (1, 2, 3)]
-        + [z_peer(x, z, t, s) for s in range(1, Z)]
+        + [z_peer(x, z, t, s) for s in (1, -1, 5, -5)]
         + [y_peer(x, z, t, s) for s in (1, 2, 3)]
         + [core_peer(x, z, t)]
     )
     bring = pltpu.make_async_copy(hidden, hidden_raw, local_sem.at[0])
     bring.start()
     own[...] = masters[...].astype(BF16)
-    spot = (z * 2 + lax.rem(x, 2), slice(None), pl.ds(pl.multiple_of(x // 2 * B, B), B))
-    weights[spot] = own[...]
+    spot = (z, lax.rem(x, 2), slice(None), pl.ds(pl.multiple_of(x // 2 * B, B), B))
+    low[spot] = own[:LOW]
+    high[x, z] = own[LOW:]
     for j in range(8):
         feats[t * 8 + j] = tokens[:, j * B : j * B + B]
     my_feats = feats.at[pl.ds(t * 8, 8)]
     wait_all()
 
+    def at_z(offset):
+        return lax.rem(z + offset + Z, Z)
+
+    def low_copy(m):
+        offset, step = MOVES[m]
+        chunk = low.at[at_z(offset)]
+        if m in STAGES[3]:
+            chunk = low.at[at_z(offset), m - STAGES[3][0]]
+        return send(chunk, chunk, zs.at[m], zr.at[m], z_peer(x, z, t, step))
+
+    def high_copy(m):
+        offset, step = MOVES[m]
+        chunk = high.at[x, at_z(offset)]
+        if m in STAGES[3]:
+            cut = (B - LOW) // 32 * 16
+            rows_m = pl.ds(0, cut) if m == STAGES[3][0] else pl.ds(cut, B - LOW - cut)
+            chunk = high.at[x, at_z(offset), rows_m]
+        return send(chunk, chunk, hs.at[m], hr.at[m], z_peer(x, z, t, step))
+
+    def high_x(offset, s):
+        chunk = high.at[x, at_z(offset)]
+        return send(chunk, chunk, hxs.at[offset % Z, s - 1], hxr.at[offset % Z, s - 1], x_peer(x, z, t, s))
+
+    sent = []
+
+    def go(copies):
+        for copy in copies:
+            copy.start()
+            sent.append(copy)
+
+    def spread_x(offsets):
+        for offset in offsets:
+            go([high_x(offset, s) for s in (1, 3, 2)])
+
+    def arrive(make, stage):
+        for m in STAGES[stage]:
+            make(m).wait_recv()
+
+    def advance(make, stage):
+        go([make(m) for m in STAGES[stage]])
+
     first = [
-        send(own, weights.at[spot], xs.at[s - 1], xr.at[s - 1], x_peer(x, z, t, s))
+        send(own.at[pl.ds(0, LOW)], low.at[spot], xs.at[s - 1], xr.at[s - 1], x_peer(x, z, t, s))
         for s in (1, 3, 2)
     ]
-    for copy in first:
-        copy.start()
+    go(first)
+    advance(high_copy, 0)
     y_moves = {
         s: send(my_feats, my_feats, ys.at[s - 1], yr.at[s - 1], y_peer(x, z, t, s))
         for s in (1, 3, 2)
     }
-    for copy in y_moves.values():
-        copy.start()
+    go(y_moves.values())
     over = send(my_feats, my_feats, cs.at[0], cr.at[0], core_peer(x, z, t))
-    over.start()
+    go([over])
+    spread_x((0,))
 
     order, row_s, col_s, upto, keep, inverse = tables(rows[...], columns[...], owners[...])
     for r, value in enumerate((order, row_s, col_s, upto, keep)):
@@ -143,67 +193,54 @@
 
     for copy in first:
         copy.wait_recv()
-
-    def hop(way, step, half):
-        sign = 1 - 2 * way
-        index = lax.rem(z - sign * step + 2 * Z, Z) * 2 + half
-        return send(
-            weights.at[index], weights.at[index],
-            zs.at[way, step, half], zr.at[way, step, half], z_peer(x, z, t, sign),
-        )
-
-    def hops(step):
-        if step < 7:
-            return [(way, half) for half in (0, 1) for way in (0, 1)]
-        return [(0, 0), (1, 1)]
-
-    def forward(step, half):
-        zz = lax.rem(z + step + 2 * Z, Z)
-        spot_k = half * Z + zz
-        raw[spot_k] = jnp.dot(
-            feats[meta[6, spot_k]], weights[zz * 2 + half], preferred_element_type=F32
-        )
-
-    sent = []
+    advance(low_copy, 0)
+    arrive(high_copy, 0)
+    advance(high_copy, 1)
+    spread_x((-5, 5, -1, 1))
+    bring.wait()
+    for c in range(hid.shape[0]):
+        hid[c] = hidden_raw[:, c * B : c * B + B]
+    arrive(low_copy, 0)
+    advance(low_copy, 1)
+    arrive(high_copy, 1)
+    advance(high_copy, 2)
+    spread_x((-6, -4, 4, 6, -2, 2))
+    arrive(low_copy, 1)
+    advance(low_copy, 2)
+    arrive(high_copy, 2)
+    advance(high_copy, 3)
+    spread_x((-7, 3, -3, 7))
+
     passed = []
-    for step in range(8):
-        now = []
-        for way, half in hops(step):
-            if step:
-                hop(way, step - 1, half).wait_recv()
-            copy = hop(way, step, half)
-            copy.start()
-            now.append(copy)
-        if step == 7:
-            for way, half in ((0, 1), (1, 0)):
-                hop(way, 6, half).wait_recv()
-        sent += now
-        if step == 0:
-            bring.wait()
-            for c in range(hid.shape[0]):
-                hid[c] = hidden_raw[:, c * B : c * B + B]
-        if step == 1:
-            to_scalar.wait()
-        if step in (3, 4, 5):
-            s = {3: 1, 4: 3, 5: 2}[step]
-            y_moves[s].wait_recv()
-            source = feats.at[pl.ds(lax.rem(t - CORES * s + Y * CORES, Y * CORES) * 8, 8)]
-            copy = send(source, source, cs.at[s], cr.at[s], core_peer(x, z, t))
-            copy.start()
-            passed.append(copy)
-        if step == 6:
-            over.wait_recv()
-            for copy in passed:
-                copy.wait_recv()
-        if step >= 6:
-            early = [0, 1, -1, 2, -2, 3, -3] if step == 6 else [4, -4, 5, -5, 6, -6, 7, -7]
-            for distance in early:
-                for half in range(2):
-                    forward(distance, half)
-    for copy in now:
+    for s in (1, 3, 2):
+        y_moves[s].wait_recv()
+        source = feats.at[pl.ds(lax.rem(t - CORES * s + Y * CORES, Y * CORES) * 8, 8)]
+        copy = send(source, source, cs.at[s], cr.at[s], core_peer(x, z, t))
+        go([copy])
+        passed.append(copy)
+    arrive(low_copy, 2)
+    advance(low_copy, 3)
+    arrive(high_copy, 3)
+    spread_x((8,))
+    to_scalar.wait()
+    over.wait_recv()
+    for copy in passed:
         copy.wait_recv()
-    for half in range(2):
-        forward(8, half)
+
+    def forward(offset):
+        for s in (1, 3, 2):
+            high_x(offset, s).wait_recv()
+        zz = at_z(offset)
+        for half in range(2):
+            spot_k = half * Z + zz
+            top = jnp.concatenate([high[half, zz], high[half + 2, zz]], axis=1)
+            weight = jnp.concatenate([low[zz, half], top], axis=0)
+            raw[spot_k] = jnp.dot(feats[meta[6, spot_k]], weight, preferred_element_type=F32)
+
+    for offset in (0, -5, 5, -1, 1, -6, -4, 4, 6, -2, 2, -7, 3, -3, 7):
+        forward(offset)
+    arrive(low_copy, 3)
+    forward(8)
 
     part[0] = jnp.zeros_like(part[0])
 
@@ -367,8 +404,7 @@
     out[:, block_rows] = final_out[x]
     for copy in final:
         copy.wait_recv()
-    done = first + list(y_moves.values()) + [over] + passed + sent
-    done += sum(a_copies, []) + sum(b_copies, []) + second + owner_copies + final
+    done = sent + sum(a_copies, []) + sum(b_copies, []) + second + owner_copies + final
     for copy in done:
         copy.wait_send()
 
@@ -385,7 +421,8 @@
         scratch_shapes=[
             pltpu.VMEM((B, B), BF16),
             pltpu.VMEM((Y * CORES * 8, B, B), BF16),
-            pltpu.VMEM((KP, B, 2 * B), BF16),
+            pltpu.VMEM((Z, 2, LOW, 2 * B), BF16),
+            pltpu.VMEM((X, Z, B - LOW, B), BF16),
             pltpu.VMEM(hidden_grad.shape, BF16),
             pltpu.VMEM((columns, B, B), BF16),
             pltpu.VMEM((8, 2 * B), jnp.int32),
@@ -406,7 +443,8 @@
             pltpu.VMEM((Z, 96, B), BF16),
             pltpu.VMEM((X, CAP, 32, B), F32),
             DMA((2,)),
-            DMA((3,)), DMA((3,)), DMA((2, 8, 2)), DMA((2, 8, 2)), DMA((3,)), DMA((3,)), DMA((4,)), DMA((4,)),
+            DMA((3,)), DMA((3,)), DMA((Z,)), DMA((Z,)), DMA((Z,)), DMA((Z,)), DMA((Z, 3)), DMA((Z, 3)),
+            DMA((3,)), DMA((3,)), DMA((4,)), DMA((4,)),
             DMA((4, 3)), DMA((4, 3)), DMA((4, 3)), DMA((4, 3)), DMA((4,)), DMA((4,)), DMA((3,)), DMA((3,)),
             DMA((Z,)), DMA((Z,)), DMA((3,)), DMA((3,)),
         ],

time: 99 us -> 89.5 us (0.904)
  Pallas kernels: 95.8 us -> 87.1 us
    pallas_call x1, Pallas kernels: 95.8 us -> 87.1 us  [local(): pl.pallas_call(fused, name='fused', out_shape=jax.ShapeDtypeStruct((CAP,...]
where the time goes in v3:
time: 89.5 us; the launch traced here: 88.7 us
  Pallas kernels  87.1 us (97%)
  local copies, waits for them, and re-layouts  1.62 us (2%)
    pallas_call x1, Pallas kernels, local(): pl.pallas_call(fused, name='fused', out_shape=jax.ShapeDtypeStruct((CAP,...  87.1 us

profile of v3, /device:TPU:24, one launch (start us, length us, event | category | flops | bytes accessed | tf_op | source)
XLA Modules:
  0.0 88.7 jit_solution(1015008092517297327)
XLA Ops:
  0.0 87.1 %fused.1 = f32[3,128,128]{2,1,0:T(8,128)} custom-call(bf16[128,1024]{1,0:T(8,128)(2,1)} %tokens.1, bf16[128,3584]{1,0:T(8,128)(2,1)} %hidden.1, f32[128,128]{1,0:T(8,128)} %bitcast.3, s32[1,32]{1,0:T(1,128)} %rows.1, s32[1,32]{1,0:T(1,128)} %columns.1, s32[1,64]{1,0:T(1,128)} %owners.1), custom_call_target="tpu_custom_call" | custom-call | tf_op jit(solution)/shard_map/fused/pallas_call | solution.py:415
  87.1 1.6 %copy.8 = f32[1,3,128,128]{3,2,1,0:T(8,128)} copy(f32[1,3,128,128]{3,2,1,0:T(8,128)} %bitcast.2) | data formatting | bytes 393216

commit v4 on v3

--- a/solution.py
+++ b/solution.py
@@ -17,16 +17,17 @@
 SMEM = pl.BlockSpec(memory_space=pltpu.SMEM)
 DMA = pltpu.SemaphoreType.DMA
 STEPS = (2, 1, -1, 0)
+FAR = (6, 7, 8)
 XSTEPS = (2, 1, 3, 0)
-HALF = KP // 2
+FIRST = 18
 LOW = 32
 MOVES = (
     (0, 5), (0, -5), (0, 1), (0, -1),
     (-5, 1), (-5, -1), (5, 1), (5, -1), (-1, 1), (1, -1),
-    (-6, 1), (4, 1), (-4, -1), (6, -1),
-    (-7, 1), (7, -1),
+    (-6, 2), (6, -2), (-6, 1), (4, 1), (-4, -1), (6, -1),
 )
-STAGES = ((0, 1, 2, 3), (4, 5, 6, 7, 8, 9), (10, 11, 12, 13), (14, 15))
+STAGES = ((0, 1, 2, 3), (4, 5, 6, 7, 8, 9), (10, 11, 12, 13, 14, 15))
+HALVES = (10, 11)
 
 
 def place():
@@ -104,10 +105,10 @@
 
 def fused(
     tokens, hidden, masters, rows, columns, owners, out,
-    own, feats, low, high, hidden_raw, hid, table, meta, raw, part, grads,
-    part_a, part_b, in_a, in_b, out_a, out_b, in_a2, in_b2, mine, owner_out, owner_in, final_out,
+    own, feats, low, high, hidden_raw, hid, table, meta, raw, part,
+    part_a, part_b, in_a, in_b, out_a, out_b, in_a2, in_b2, mine, owner_out, owner_in, relay_in, final_out,
     local_sem, xs, xr, zs, zr, hs, hr, hxs, hxr, ys, yr, cs, cr,
-    as_, ar, bs, br, as2, ar2, bs2, br2, os, ors, fs, fr,
+    as_, ar, bs, br, as2, ar2, bs2, br2, os, ors, rs, rr, fs, fr,
 ):
     x, z, t = place()
     wait_all = greet(
@@ -133,16 +134,16 @@
     def low_copy(m):
         offset, step = MOVES[m]
         chunk = low.at[at_z(offset)]
-        if m in STAGES[3]:
-            chunk = low.at[at_z(offset), m - STAGES[3][0]]
+        if m in HALVES:
+            chunk = low.at[at_z(offset), m - HALVES[0]]
         return send(chunk, chunk, zs.at[m], zr.at[m], z_peer(x, z, t, step))
 
     def high_copy(m):
         offset, step = MOVES[m]
         chunk = high.at[x, at_z(offset)]
-        if m in STAGES[3]:
+        if m in HALVES:
             cut = (B - LOW) // 32 * 16
-            rows_m = pl.ds(0, cut) if m == STAGES[3][0] else pl.ds(cut, B - LOW - cut)
+            rows_m = pl.ds(0, cut) if m == HALVES[0] else pl.ds(cut, B - LOW - cut)
             chunk = high.at[x, at_z(offset), rows_m]
         return send(chunk, chunk, hs.at[m], hr.at[m], z_peer(x, z, t, step))
 
@@ -208,8 +209,7 @@
     arrive(low_copy, 1)
     advance(low_copy, 2)
     arrive(high_copy, 2)
-    advance(high_copy, 3)
-    spread_x((-7, 3, -3, 7))
+    spread_x((-7, 3, -3, 7, 8))
 
     passed = []
     for s in (1, 3, 2):
@@ -218,10 +218,6 @@
         copy = send(source, source, cs.at[s], cr.at[s], core_peer(x, z, t))
         go([copy])
         passed.append(copy)
-    arrive(low_copy, 2)
-    advance(low_copy, 3)
-    arrive(high_copy, 3)
-    spread_x((8,))
     to_scalar.wait()
     over.wait_recv()
     for copy in passed:
@@ -237,9 +233,11 @@
             weight = jnp.concatenate([low[zz, half], top], axis=0)
             raw[spot_k] = jnp.dot(feats[meta[6, spot_k]], weight, preferred_element_type=F32)
 
-    for offset in (0, -5, 5, -1, 1, -6, -4, 4, 6, -2, 2, -7, 3, -3, 7):
+    for offset in (0, -5, 5, -1, 1, -6, -4, 4, 6, -2, 2):
         forward(offset)
-    arrive(low_copy, 3)
+    arrive(low_copy, 2)
+    for offset in (-7, 3, -3, 7):
+        forward(offset)
     forward(8)
 
     part[0] = jnp.zeros_like(part[0])
@@ -255,16 +253,17 @@
         upstream = hid[meta[2, i]].astype(F32)
         sig = 1.0 / (1.0 + jnp.exp(-gate))
         scaled = upstream * sig
-        grads[:, :B] = (scaled * up * (1.0 + gate * (1.0 - sig))).astype(BF16)
-        grads[:, B:] = (scaled * gate).astype(BF16)
+        grad = jnp.concatenate(
+            [(scaled * up * (1.0 + gate * (1.0 - sig))).astype(BF16), (scaled * gate).astype(BF16)], axis=1
+        )
         block = lax.dot_general(
-            feats[meta[1, i]], grads[...], (((0,), (0,)), ((), ())), preferred_element_type=F32
+            feats[meta[1, i]], grad, (((0,), (0,)), ((), ())), preferred_element_type=F32
         )
         for p in range(16):
             r = block[8 * p : 8 * p + 8]
             store(p, jnp.concatenate([r[:, :B], r[:, B:]], axis=0).astype(BF16))
 
-    @pl.loop(0, HALF)
+    @pl.loop(0, FIRST, unroll=2)
     def _(i):
         at = pl.ds(pl.multiple_of(i * 16, 16), 16)
 
@@ -285,14 +284,14 @@
         for copy in group:
             copy.start()
 
-    @pl.loop(0, HALF)
+    @pl.loop(0, KP - FIRST, unroll=2)
     def _(i):
         at = pl.ds(pl.multiple_of(i * 16, 16), 16)
 
         def store(p, v):
             part_b[p, at] = v
 
-        backward(i + HALF, store)
+        backward(i + FIRST, store)
 
     def b_copy(j, k):
         step = STEPS[k] if k or j % 2 == 0 else -STEPS[k]
@@ -306,11 +305,10 @@
         for copy in group:
             copy.start()
 
-    tile = 64
-    size = HALF * 16
-
-    def merge(own_piece, arrived, store):
-        @pl.loop(0, size // tile)
+    tile = 32
+
+    def merge(count, own_piece, arrived, store):
+        @pl.loop(0, count * 16 // tile)
         def _(r):
             at = pl.ds(pl.multiple_of(r * tile, tile), tile)
             value = own_piece[at].astype(F32)
@@ -324,23 +322,23 @@
             if j < 3:
                 out_a[j, at] = value.astype(BF16)
             else:
-                mine[pl.ds(r * 8, 8)] = value.reshape(8, 8, B)
+                mine[pl.ds(r * 4, 4)] = value.reshape(4, 8, B)
 
         def keep_b(r, at, value, j=j):
             if j < 3:
                 out_b[j, at] = value.astype(BF16)
             else:
-                mine[pl.ds(KP + r * 8, 8)] = value.reshape(8, 8, B)
+                mine[pl.ds(2 * FIRST + r * 4, 4)] = value.reshape(4, 8, B)
 
         for copy in a_copies[j]:
             copy.wait_recv()
-        merge(part_a.at[x * 4 + lax.rem(z + STEPS[j] + Z, 4)], in_a.at[j], keep_a)
+        merge(FIRST, part_a.at[x * 4 + lax.rem(z + STEPS[j] + Z, 4)], in_a.at[j], keep_a)
         if j < 3:
             if j == 0:
-                cut = size // 2
-                pieces = [(pl.ds(0, cut), 0, 2), (pl.ds(cut, cut), 3, -2)]
+                cut = FIRST // 2 * 16
+                pieces = [(pl.ds(0, cut), 0, 2), (pl.ds(cut, FIRST * 16 - cut), 3, -2)]
             else:
-                pieces = [(pl.ds(0, size), j, STEPS[j])]
+                pieces = [(pl.ds(0, FIRST * 16), j, STEPS[j])]
             for at, sem, step in pieces:
                 copy = send(out_a.at[j, at], in_a2.at[j, at], as2.at[sem], ar2.at[sem],
                             z_peer(x, z, t, step))
@@ -348,7 +346,7 @@
                 second.append(copy)
         for copy in b_copies[j]:
             copy.wait_recv()
-        merge(part_b.at[lax.rem(x + XSTEPS[j], X) * 4 + lax.rem(z, 4)], in_b.at[j], keep_b)
+        merge(KP - FIRST, part_b.at[lax.rem(x + XSTEPS[j], X) * 4 + lax.rem(z, 4)], in_b.at[j], keep_b)
         if j < 3:
             copy = send(out_b.at[j], in_b2.at[j], bs2.at[j], br2.at[j], x_peer(x, z, t, XSTEPS[j]))
             copy.start()
@@ -356,40 +354,83 @@
     for copy in second:
         copy.wait_recv()
 
-    for base, arrived in ((0, in_a2), (KP, in_b2)):
-        @pl.loop(0, size // tile)
+    for base, count, arrived in ((0, FIRST, in_a2), (2 * FIRST, KP - FIRST, in_b2)):
+        @pl.loop(0, count * 16 // tile)
         def _(r):
             at = pl.ds(pl.multiple_of(r * tile, tile), tile)
-            blocks = pl.ds(base + r * 8, 8)
+            blocks = pl.ds(base + r * 4, 4)
             value = mine[blocks].reshape(tile, B)
             for j in range(3):
                 value += arrived[j, at].astype(F32)
-            mine[blocks] = value.reshape(8, 8, B)
+            mine[blocks] = value.reshape(4, 8, B)
 
     mine[2 * KP] = jnp.zeros((8, B), F32)
 
     def slot(zo, q):
         return mine[meta[5, (q // CAP * Z + zo) * CAP + q % CAP]]
 
-    owner_copies = []
-    for step in (8, 7, 9, 6, 10, 5, 11, 4, 12, 3, 13, 2, 14, 1, 15, 0):
-        zo = lax.rem(z + step, Z)
+    def collect(step):
+        zo = lax.rem(z + step + Z, Z)
         for q in range(0, 12, 2):
-            owner_out[step, 8 * q : 8 * q + 16] = jnp.concatenate(
+            owner_out[step % Z, 8 * q : 8 * q + 16] = jnp.concatenate(
                 [slot(zo, q), slot(zo, q + 1)], axis=0
             ).astype(BF16)
-        if step:
-            copy = send(owner_out.at[step], owner_in.at[step], os.at[step], ors.at[step],
-                        z_peer(x, z, t, step))
+
+    half_rows = 48
+
+    def share(step, way):
+        if step < 8:
+            return pl.ds(0, 96)
+        return pl.ds(0 if way > 0 else half_rows, half_rows)
+
+    def relay(step, way):
+        k = step - FAR[0] + (0 if way > 0 else len(FAR))
+        at = share(step, way)
+        return send(owner_out.at[step * way % Z, at], relay_in.at[k, at], rs.at[k], rr.at[k],
+                    z_peer(x, z, t, 4 * way))
+
+    def direct(step, way):
+        k = step * way % Z
+        return send(owner_out.at[k], owner_in.at[k], os.at[k], ors.at[k], z_peer(x, z, t, step * way))
+
+    owner_copies = []
+    for step in FAR:
+        for way in (1, -1):
+            if step < 8 or way > 0:
+                collect(step * way)
+            copy = relay(step, way)
             copy.start()
             owner_copies.append(copy)
-    for copy in owner_copies:
+    arrivals = []
+    for step in (5, 1):
+        for way in (1, -1):
+            collect(step * way)
+            copy = direct(step, way)
+            copy.start()
+            arrivals.append(copy)
+    for step in (2, 3, 4):
+        for way in (1, -1):
+            collect(step * way)
+    collect(0)
+    for step in (2, 3, 4):
+        for way in (1, -1):
+            relay(step + 4, way).wait_recv()
+            at = share(step + 4, way)
+            k = step - 2 + (0 if way > 0 else len(FAR))
+            near_sum = owner_out[step * way % Z, at].astype(F32) + relay_in[k, at].astype(F32)
+            owner_out[step * way % Z, at] = near_sum.astype(BF16)
+            copy = direct(step, way)
+            copy.start()
+            arrivals.append(copy)
+    for copy in arrivals:
         copy.wait_recv()
+    owner_copies += arrivals
     for e in range(4):
-        value = owner_out[0] if e == 0 else owner_in[e]
-        value = value.astype(F32)
-        for k in (4, 8, 12):
-            value += owner_in[e + k].astype(F32)
+        near = {0: (4, 12), 1: (1, 5, 13), 2: (2, 14), 3: (3, 15, 11)}[e]
+        value = owner_out[0].astype(F32) if e == 0 else None
+        for k in near:
+            more = owner_in[k].astype(F32)
+            value = more if value is None else value + more
         row = pl.multiple_of(lax.rem(z - e + Z, 4) * 8, 8)
         for q in range(12):
             final_out[q // CAP, q % CAP, pl.ds(row, 8)] = value[8 * q : 8 * q + 8]
@@ -410,7 +451,7 @@
 
 
 def local(tokens, hidden_grad, masters, block_row, block_col, owners):
-    size = HALF * 16
+    size_a, size_b = FIRST * 16, (KP - FIRST) * 16
     columns = hidden_grad.shape[1] // B
     result = pl.pallas_call(
         fused,
@@ -429,24 +470,24 @@
             pltpu.SMEM((8, 2 * B), jnp.int32),
             pltpu.VMEM((KP, B, 2 * B), F32),
             pltpu.VMEM((KP + 1, B, 2 * B), F32),
-            pltpu.VMEM((B, 2 * B), BF16),
-            pltpu.VMEM((16, size, B), BF16),
-            pltpu.VMEM((16, size, B), BF16),
-            pltpu.VMEM((4, 3, size, B), BF16),
-            pltpu.VMEM((4, 3, size, B), BF16),
-            pltpu.VMEM((3, size, B), BF16),
-            pltpu.VMEM((3, size, B), BF16),
-            pltpu.VMEM((3, size, B), BF16),
-            pltpu.VMEM((3, size, B), BF16),
+            pltpu.VMEM((16, size_a, B), BF16),
+            pltpu.VMEM((16, size_b, B), BF16),
+            pltpu.VMEM((4, 3, size_a, B), BF16),
+            pltpu.VMEM((4, 3, size_b, B), BF16),
+            pltpu.VMEM((3, size_a, B), BF16),
+            pltpu.VMEM((3, size_b, B), BF16),
+            pltpu.VMEM((3, size_a, B), BF16),
+            pltpu.VMEM((3, size_b, B), BF16),
             pltpu.VMEM((2 * KP + 1, 8, B), F32),
             pltpu.VMEM((Z, 96, B), BF16),
             pltpu.VMEM((Z, 96, B), BF16),
+            pltpu.VMEM((6, 96, B), BF16),
             pltpu.VMEM((X, CAP, 32, B), F32),
             DMA((2,)),
             DMA((3,)), DMA((3,)), DMA((Z,)), DMA((Z,)), DMA((Z,)), DMA((Z,)), DMA((Z, 3)), DMA((Z, 3)),
             DMA((3,)), DMA((3,)), DMA((4,)), DMA((4,)),
             DMA((4, 3)), DMA((4, 3)), DMA((4, 3)), DMA((4, 3)), DMA((4,)), DMA((4,)), DMA((3,)), DMA((3,)),
-            DMA((Z,)), DMA((Z,)), DMA((3,)), DMA((3,)),
+            DMA((Z,)), DMA((Z,)), DMA((6,)), DMA((6,)), DMA((3,)), DMA((3,)),
         ],
         compiler_params=pltpu.CompilerParams(
             collective_id=0, has_side_effects=True, vmem_limit_bytes=56 << 20

time: 89.5 us -> 85.9 us (0.960)
  Pallas kernels: 87.1 us -> 83.5 us
    pallas_call x1, Pallas kernels: 87.1 us -> 83.5 us  [local(): pl.pallas_call(fused, name='fused', out_shape=jax.ShapeDtypeStruct((CAP,...]
where the time goes in v4:
time: 85.9 us; the launch traced here: 85.1 us
  Pallas kernels  83.5 us (97%)
  local copies, waits for them, and re-layouts  1.62 us (2%)
    pallas_call x1, Pallas kernels, local(): pl.pallas_call(fused, name='fused', out_shape=jax.ShapeDtypeStruct((CAP,...  83.5 us

profile of v4, /device:TPU:24, one launch (start us, length us, event | category | flops | bytes accessed | tf_op | source)
XLA Modules:
  0.0 85.1 jit_solution(5618159985295944009)
XLA Ops:
  0.0 83.5 %fused.1 = f32[3,128,128]{2,1,0:T(8,128)} custom-call(bf16[128,1024]{1,0:T(8,128)(2,1)} %tokens.1, bf16[128,3584]{1,0:T(8,128)(2,1)} %hidden.1, f32[128,128]{1,0:T(8,128)} %bitcast.3, s32[1,32]{1,0:T(1,128)} %rows.1, s32[1,32]{1,0:T(1,128)} %columns.1, s32[1,64]{1,0:T(1,128)} %owners.1), custom_call_target="tpu_custom_call" | custom-call | tf_op jit(solution)/shard_map/fused/pallas_call | solution.py:456
  83.5 1.6 %copy.8 = f32[1,3,128,128]{3,2,1,0:T(8,128)} copy(f32[1,3,128,128]{3,2,1,0:T(8,128)} %bitcast.2) | data formatting | bytes 393216

commit v5 on v4

--- a/solution.py
+++ b/solution.py
@@ -17,9 +17,9 @@
 SMEM = pl.BlockSpec(memory_space=pltpu.SMEM)
 DMA = pltpu.SemaphoreType.DMA
 STEPS = (2, 1, -1, 0)
-FAR = (6, 7, 8)
+FAR = (7, 8,)
 XSTEPS = (2, 1, 3, 0)
-FIRST = 18
+FIRST = 16
 LOW = 32
 MOVES = (
     (0, 5), (0, -5), (0, 1), (0, -1),
@@ -242,7 +242,7 @@
 
     part[0] = jnp.zeros_like(part[0])
 
-    @pl.loop(0, KP)
+    @pl.loop(0, KP, unroll=4)
     def _(i):
         part[i + 1] = part[i] * meta[4, i].astype(F32) + raw[meta[0, i]]
 
@@ -263,7 +263,7 @@
             r = block[8 * p : 8 * p + 8]
             store(p, jnp.concatenate([r[:, :B], r[:, B:]], axis=0).astype(BF16))
 
-    @pl.loop(0, FIRST, unroll=2)
+    @pl.loop(0, FIRST, unroll=8)
     def _(i):
         at = pl.ds(pl.multiple_of(i * 16, 16), 16)
 
@@ -284,7 +284,7 @@
         for copy in group:
             copy.start()
 
-    @pl.loop(0, KP - FIRST, unroll=2)
+    @pl.loop(0, KP - FIRST, unroll=8)
     def _(i):
         at = pl.ds(pl.multiple_of(i * 16, 16), 16)
 
@@ -316,6 +316,8 @@
                 value += arrived[k, at].astype(F32)
             store(r, at, value)
 
+    for copy in sent:
+        copy.wait_send()
     second = []
     for j in range(4):
         def keep_a(r, at, value, j=j):
@@ -402,31 +404,33 @@
             copy.start()
             owner_copies.append(copy)
     arrivals = []
-    for step in (5, 1):
+    for step in (6, 5, 2, 1,):
         for way in (1, -1):
             collect(step * way)
             copy = direct(step, way)
             copy.start()
             arrivals.append(copy)
-    for step in (2, 3, 4):
+    for step in (3, 4,):
         for way in (1, -1):
             collect(step * way)
     collect(0)
-    for step in (2, 3, 4):
+    for step in (3, 4,):
         for way in (1, -1):
             relay(step + 4, way).wait_recv()
             at = share(step + 4, way)
-            k = step - 2 + (0 if way > 0 else len(FAR))
+            k = step - 3 + (0 if way > 0 else len(FAR))
             near_sum = owner_out[step * way % Z, at].astype(F32) + relay_in[k, at].astype(F32)
             owner_out[step * way % Z, at] = near_sum.astype(BF16)
             copy = direct(step, way)
             copy.start()
             arrivals.append(copy)
+    for copy in sum(a_copies, []) + sum(b_copies, []) + second:
+        copy.wait_send()
     for copy in arrivals:
         copy.wait_recv()
     owner_copies += arrivals
     for e in range(4):
-        near = {0: (4, 12), 1: (1, 5, 13), 2: (2, 14), 3: (3, 15, 11)}[e]
+        near = {0: (4, 12), 1: (1, 5, 13), 2: (2, 6, 10, 14), 3: (3, 11, 15)}[e]
         value = owner_out[0].astype(F32) if e == 0 else None
         for k in near:
             more = owner_in[k].astype(F32)
@@ -445,7 +449,7 @@
     out[:, block_rows] = final_out[x]
     for copy in final:
         copy.wait_recv()
-    done = sent + sum(a_copies, []) + sum(b_copies, []) + second + owner_copies + final
+    done = owner_copies + final
     for copy in done:
         copy.wait_send()
 
@@ -481,13 +485,13 @@
             pltpu.VMEM((2 * KP + 1, 8, B), F32),
             pltpu.VMEM((Z, 96, B), BF16),
             pltpu.VMEM((Z, 96, B), BF16),
-            pltpu.VMEM((6, 96, B), BF16),
+            pltpu.VMEM((4, 96, B), BF16),
             pltpu.VMEM((X, CAP, 32, B), F32),
             DMA((2,)),
             DMA((3,)), DMA((3,)), DMA((Z,)), DMA((Z,)), DMA((Z,)), DMA((Z,)), DMA((Z, 3)), DMA((Z, 3)),
             DMA((3,)), DMA((3,)), DMA((4,)), DMA((4,)),
             DMA((4, 3)), DMA((4, 3)), DMA((4, 3)), DMA((4, 3)), DMA((4,)), DMA((4,)), DMA((3,)), DMA((3,)),
-            DMA((Z,)), DMA((Z,)), DMA((6,)), DMA((6,)), DMA((3,)), DMA((3,)),
+            DMA((Z,)), DMA((Z,)), DMA((4,)), DMA((4,)), DMA((3,)), DMA((3,)),
         ],
         compiler_params=pltpu.CompilerParams(
             collective_id=0, has_side_effects=True, vmem_limit_bytes=56 << 20

time: 85.9 us -> 82.8 us (0.964)
  Pallas kernels: 83.5 us -> 79.9 us
    pallas_call x1, Pallas kernels: 83.5 us -> 79.9 us  [local(): pl.pallas_call(fused, name='fused', out_shape=jax.ShapeDtypeStruct((CAP,...]
where the time goes in v5:
time: 82.8 us; the launch traced here: 81.5 us
  Pallas kernels  79.9 us (96%)
  local copies, waits for them, and re-layouts  1.62 us (2%)
    pallas_call x1, Pallas kernels, local(): pl.pallas_call(fused, name='fused', out_shape=jax.ShapeDtypeStruct((CAP,...  79.9 us

profile of v5, /device:TPU:24, one launch (start us, length us, event | category | flops | bytes accessed | tf_op | source)
XLA Modules:
  0.0 81.5 jit_solution(1699245049443495096)
XLA Ops:
  0.0 79.9 %fused.1 = f32[3,128,128]{2,1,0:T(8,128)} custom-call(bf16[128,1024]{1,0:T(8,128)(2,1)} %tokens.1, bf16[128,3584]{1,0:T(8,128)(2,1)} %hidden.1, f32[128,128]{1,0:T(8,128)} %bitcast.3, s32[1,32]{1,0:T(1,128)} %rows.1, s32[1,32]{1,0:T(1,128)} %columns.1, s32[1,64]{1,0:T(1,128)} %owners.1), custom_call_target="tpu_custom_call" | custom-call | tf_op jit(solution)/shard_map/fused/pallas_call | solution.py:460
  79.9 1.6 %copy.8 = f32[1,3,128,128]{3,2,1,0:T(8,128)} copy(f32[1,3,128,128]{3,2,1,0:T(8,128)} %bitcast.2) | data formatting | bytes 393216

commit v6 on v5

--- a/solution.py
+++ b/solution.py
@@ -460,7 +460,7 @@
     result = pl.pallas_call(
         fused,
         name="fused",
-        out_shape=jax.ShapeDtypeStruct((CAP, B, B), F32),
+        out_shape=pltpu.VMEM((CAP, B, B), F32),
         in_specs=[VMEM, pl.BlockSpec(memory_space=pl.ANY), VMEM, VMEM, VMEM, VMEM],
         out_specs=VMEM,
         scratch_shapes=[

time: 82.8 us -> 81.2 us (0.981)
  local copies, waits for them, and re-layouts: 1.62 us -> 0.68 us
    unnamed x1, local copies, waits for them, and re-layouts: 1.62 us -> 0.68 us
where the time goes in v6:
time: 81.2 us; the launch traced here: 79.8 us
  Pallas kernels  79.2 us (98%)
    pallas_call x1, Pallas kernels, local(): pl.pallas_call(fused, name='fused', out_shape=pltpu.VMEM((CAP, B, B), F32...  79.2 us

profile of v6, /device:TPU:24, one launch (start us, length us, event | category | flops | bytes accessed | tf_op | source)
XLA Modules:
  0.0 79.8 jit_solution(2960804110617384640)
XLA Ops:
  0.0 79.2 %fused.1 = f32[3,128,128]{2,1,0:T(8,128)S(1)} custom-call(bf16[128,1024]{1,0:T(8,128)(2,1)} %tokens.1, bf16[128,3584]{1,0:T(8,128)(2,1)} %hidden.1, f32[128,128]{1,0:T(8,128)} %bitcast.3, s32[1,32]{1,0:T(1,128)} %rows.1, s32[1,32]{1,0:T(1,128)} %columns.1, s32[1,64]{1,0:T(1,128)} %owners.1), custom_call_target="tpu_custom_call" | custom-call | tf_op jit(solution)/shard_map/fused/pallas_call | solution.py:460
  79.2 0.7 copy.8

commit v7 on v6

--- a/solution.py
+++ b/solution.py
@@ -14,7 +14,7 @@
 CAP = 3
 F32, BF16 = jnp.float32, jnp.bfloat16
 VMEM = pl.BlockSpec(memory_space=pltpu.VMEM)
-SMEM = pl.BlockSpec(memory_space=pltpu.SMEM)
+ANY = pl.BlockSpec(memory_space=pl.ANY)
 DMA = pltpu.SemaphoreType.DMA
 STEPS = (2, 1, -1, 0)
 FAR = (7, 8,)
@@ -104,8 +104,8 @@
 
 
 def fused(
-    tokens, hidden, masters, rows, columns, owners, out,
-    own, feats, low, high, hidden_raw, hid, table, meta, raw, part,
+    tokens, hidden, masters, rows_in, columns_in, owners_in, out,
+    rows, columns, owners, own, feats, low, high, masters_raw, tokens_raw, hidden_raw, hid, table, meta, raw, part,
     part_a, part_b, in_a, in_b, out_a, out_b, in_a2, in_b2, mine, owner_out, owner_in, relay_in, final_out,
     local_sem, xs, xr, zs, zr, hs, hr, hxs, hxr, ys, yr, cs, cr,
     as_, ar, bs, br, as2, ar2, bs2, br2, os, ors, rs, rr, fs, fr,
@@ -118,13 +118,25 @@
         + [core_peer(x, z, t)]
     )
     bring = pltpu.make_async_copy(hidden, hidden_raw, local_sem.at[0])
+    bring_small = [
+        pltpu.make_async_copy(source, target, local_sem.at[4 + k])
+        for k, (source, target) in enumerate(((rows_in, rows), (columns_in, columns), (owners_in, owners)))
+    ]
+    bring_masters = pltpu.make_async_copy(masters, masters_raw, local_sem.at[2])
+    bring_tokens = pltpu.make_async_copy(tokens, tokens_raw, local_sem.at[3])
+    bring_masters.start()
+    bring_tokens.start()
     bring.start()
-    own[...] = masters[...].astype(BF16)
+    for copy in bring_small:
+        copy.start()
+    bring_masters.wait()
+    own[...] = masters_raw[...].astype(BF16)
     spot = (z, lax.rem(x, 2), slice(None), pl.ds(pl.multiple_of(x // 2 * B, B), B))
     low[spot] = own[:LOW]
     high[x, z] = own[LOW:]
+    bring_tokens.wait()
     for j in range(8):
-        feats[t * 8 + j] = tokens[:, j * B : j * B + B]
+        feats[t * 8 + j] = tokens_raw[:, j * B : j * B + B]
     my_feats = feats.at[pl.ds(t * 8, 8)]
     wait_all()
 
@@ -184,6 +196,8 @@
     go([over])
     spread_x((0,))
 
+    for copy in bring_small:
+        copy.wait()
     order, row_s, col_s, upto, keep, inverse = tables(rows[...], columns[...], owners[...])
     for r, value in enumerate((order, row_s, col_s, upto, keep)):
         table[r : r + 1, :B] = value
@@ -461,13 +475,18 @@
         fused,
         name="fused",
         out_shape=pltpu.VMEM((CAP, B, B), F32),
-        in_specs=[VMEM, pl.BlockSpec(memory_space=pl.ANY), VMEM, VMEM, VMEM, VMEM],
+        in_specs=[ANY, ANY, ANY, ANY, ANY, ANY],
         out_specs=VMEM,
         scratch_shapes=[
+            pltpu.VMEM(block_row.shape, jnp.int32),
+            pltpu.VMEM(block_col.shape, jnp.int32),
+            pltpu.VMEM(owners.shape, jnp.int32),
             pltpu.VMEM((B, B), BF16),
             pltpu.VMEM((Y * CORES * 8, B, B), BF16),
             pltpu.VMEM((Z, 2, LOW, 2 * B), BF16),
             pltpu.VMEM((X, Z, B - LOW, B), BF16),
+            pltpu.VMEM((B, B), F32),
+            pltpu.VMEM(tokens.shape, BF16),
             pltpu.VMEM(hidden_grad.shape, BF16),
             pltpu.VMEM((columns, B, B), BF16),
             pltpu.VMEM((8, 2 * B), jnp.int32),
@@ -487,7 +506,7 @@
             pltpu.VMEM((Z, 96, B), BF16),
             pltpu.VMEM((4, 96, B), BF16),
             pltpu.VMEM((X, CAP, 32, B), F32),
-            DMA((2,)),
+            DMA((7,)),
             DMA((3,)), DMA((3,)), DMA((Z,)), DMA((Z,)), DMA((Z,)), DMA((Z,)), DMA((Z, 3)), DMA((Z, 3)),
             DMA((3,)), DMA((3,)), DMA((4,)), DMA((4,)),
             DMA((4, 3)), DMA((4, 3)), DMA((4, 3)), DMA((4, 3)), DMA((4,)), DMA((4,)), DMA((3,)), DMA((3,)),

time: 81.2 us -> 80.3 us (0.989)
  no operation moved by 1% of the time
where the time goes in v7:
time: 80.3 us; the launch traced here: 79.7 us
  Pallas kernels  79 us (98%)
    pallas_call x1, Pallas kernels, local(): pl.pallas_call(fused, name='fused', out_shape=pltpu.VMEM((CAP, B, B), F32...  79 us

profile of v7, /device:TPU:24, one launch (start us, length us, event | category | flops | bytes accessed | tf_op | source)
XLA Modules:
  0.0 79.7 jit_solution(16893975326853411334)
XLA Ops:
  0.0 79.0 %fused.1 = f32[3,128,128]{2,1,0:T(8,128)S(1)} custom-call(bf16[128,1024]{1,0:T(8,128)(2,1)} %tokens.1, bf16[128,3584]{1,0:T(8,128)(2,1)} %hidden.1, f32[128,128]{1,0:T(8,128)} %bitcast.3, s32[1,32]{1,0:T(1,128)} %rows_in.1, s32[1,32]{1,0:T(1,128)} %columns_in.1, s32[1,64]{1,0:T(1,128)} %owners_in.1), custom_call_target="tpu_custom_call" | custom-call | tf_op jit(solution)/shard_map/fused/pallas_call | solution.py:474
  79.0 0.7 copy.8

commit v8 on v7

--- a/solution.py
+++ b/solution.py
@@ -277,7 +277,7 @@
             r = block[8 * p : 8 * p + 8]
             store(p, jnp.concatenate([r[:, :B], r[:, B:]], axis=0).astype(BF16))
 
-    @pl.loop(0, FIRST, unroll=8)
+    @pl.loop(0, FIRST, unroll=16)
     def _(i):
         at = pl.ds(pl.multiple_of(i * 16, 16), 16)
 
@@ -298,7 +298,7 @@
         for copy in group:
             copy.start()
 
-    @pl.loop(0, KP - FIRST, unroll=8)
+    @pl.loop(0, KP - FIRST, unroll=16)
     def _(i):
         at = pl.ds(pl.multiple_of(i * 16, 16), 16)
 
@@ -322,7 +322,7 @@
     tile = 32
 
     def merge(count, own_piece, arrived, store):
-        @pl.loop(0, count * 16 // tile)
+        @pl.loop(0, count * 16 // tile, unroll=4)
         def _(r):
             at = pl.ds(pl.multiple_of(r * tile, tile), tile)
             value = own_piece[at].astype(F32)
@@ -371,7 +371,7 @@
         copy.wait_recv()
 
     for base, count, arrived in ((0, FIRST, in_a2), (2 * FIRST, KP - FIRST, in_b2)):
-        @pl.loop(0, count * 16 // tile)
+        @pl.loop(0, count * 16 // tile, unroll=4)
         def _(r):
             at = pl.ds(pl.multiple_of(r * tile, tile), tile)
             blocks = pl.ds(base + r * 4, 4)

time: 80.3 us -> 79.7 us (level)
  no operation moved by 1% of the time
where the time goes in v8:
time: 79.7 us; the launch traced here: 79.6 us
  Pallas kernels  78.9 us (99%)
    pallas_call x1, Pallas kernels, local(): pl.pallas_call(fused, name='fused', out_shape=pltpu.VMEM((CAP, B, B), F32...  78.9 us

profile of v8, /device:TPU:24, one launch (start us, length us, event | category | flops | bytes accessed | tf_op | source)
XLA Modules:
  0.0 79.6 jit_solution(3768695341477503521)
XLA Ops:
  0.0 78.9 %fused.1 = f32[3,128,128]{2,1,0:T(8,128)S(1)} custom-call(bf16[128,1024]{1,0:T(8,128)(2,1)} %tokens.1, bf16[128,3584]{1,0:T(8,128)(2,1)} %hidden.1, f32[128,128]{1,0:T(8,128)} %bitcast.3, s32[1,32]{1,0:T(1,128)} %rows_in.1, s32[1,32]{1,0:T(1,128)} %columns_in.1, s32[1,64]{1,0:T(1,128)} %owners_in.1), custom_call_target="tpu_custom_call" | custom-call | tf_op jit(solution)/shard_map/fused/pallas_call | solution.py:474
  78.9 0.7 copy.8

commit v9 on v8

--- a/solution.py
+++ b/solution.py
@@ -256,7 +256,7 @@
 
     part[0] = jnp.zeros_like(part[0])
 
-    @pl.loop(0, KP, unroll=4)
+    @pl.loop(0, KP, unroll=16)
     def _(i):
         part[i + 1] = part[i] * meta[4, i].astype(F32) + raw[meta[0, i]]
 
@@ -322,7 +322,7 @@
     tile = 32
 
     def merge(count, own_piece, arrived, store):
-        @pl.loop(0, count * 16 // tile, unroll=4)
+        @pl.loop(0, count * 16 // tile, unroll=8)
         def _(r):
             at = pl.ds(pl.multiple_of(r * tile, tile), tile)
             value = own_piece[at].astype(F32)
@@ -371,7 +371,7 @@
         copy.wait_recv()
 
     for base, count, arrived in ((0, FIRST, in_a2), (2 * FIRST, KP - FIRST, in_b2)):
-        @pl.loop(0, count * 16 // tile, unroll=4)
+        @pl.loop(0, count * 16 // tile, unroll=8)
         def _(r):
             at = pl.ds(pl.multiple_of(r * tile, tile), tile)
             blocks = pl.ds(base + r * 4, 4)

time: 79.7 us -> 79.6 us (level)
  no operation moved by 1% of the time
where the time goes in v9:
time: 79.6 us; the launch traced here: 79.5 us
  Pallas kernels  78.8 us (99%)
    pallas_call x1, Pallas kernels, local(): pl.pallas_call(fused, name='fused', out_shape=pltpu.VMEM((CAP, B, B), F32...  78.8 us

profile of v9, /device:TPU:24, one launch (start us, length us, event | category | flops | bytes accessed | tf_op | source)
XLA Modules:
  0.0 79.5 jit_solution(14252871961721583419)
XLA Ops:
  0.0 78.8 %fused.1 = f32[3,128,128]{2,1,0:T(8,128)S(1)} custom-call(bf16[128,1024]{1,0:T(8,128)(2,1)} %tokens.1, bf16[128,3584]{1,0:T(8,128)(2,1)} %hidden.1, f32[128,128]{1,0:T(8,128)} %bitcast.3, s32[1,32]{1,0:T(1,128)} %rows_in.1, s32[1,32]{1,0:T(1,128)} %columns_in.1, s32[1,64]{1,0:T(1,128)} %owners_in.1), custom_call_target="tpu_custom_call" | custom-call | tf_op jit(solution)/shard_map/fused/pallas_call | solution.py:474
  78.8 0.7 copy.8
